TPU v7x, 32 devices: a whole 2x2x4 slice. The times are simulated.
32 devices in a mesh: dp: 16 (over z, y, x), tensor: 2 (over core).
Axes of the slice: x: 2, y: 2, z: 4, core: 2. Of those that a mesh axis runs over, the one named last changes fastest.
Arguments:
- tokens: bfloat16 [2, 16, 256, 768], P(None, 'dp', 'tensor'), may hold values from -6 to 6
- lengths: int32 [2, 16, 8], P(None, 'dp'), may hold values from 1 to 64, 256 in all within a row
- qkv_weight: bfloat16 [2, 3, 768, 768], P(None, None, 'dp', 'tensor'), may hold values from -0.21875 to 0.21875
- qkv_bias: bfloat16 [2, 2, 2, 384], P(None, None, 'tensor', 'dp'), may hold values from -3 to 3
- out_weight: bfloat16 [2, 768, 768], P(None, 'tensor', 'dp'), may hold values from -0.875 to 0.875
- up_weight: bfloat16 [2, 768, 3072], P(None, 'dp', 'tensor'), may hold values from -0.21875 to 0.21875
- up_bias: bfloat16 [2, 2, 1536], P(None, 'tensor', 'dp'), may hold values from -3 to 3
- down_weight: bfloat16 [2, 3072, 768], P(None, 'tensor', 'dp'), may hold values from -0.109375 to 0.109375
- norm_gains: bfloat16 [2, 2, 768], P(None, None, 'dp'), may hold values from 0.5 to 1.5
- shifts: bfloat16 [2, 4, 768], P(None, None, 'dp'), may hold values from -2 to 2
- cotangent: bfloat16 [2, 16, 256, 768], P(None, 'dp', 'tensor'), may hold values from -6 to 6
Outputs:
- out_tokens: float32 [2, 16, 256, 768], P(None, 'dp', 'tensor')
- token_grad: float32 [2, 16, 256, 768], P(None, 'dp', 'tensor')
- qkv_weight_grad: float32 [2, 3, 768, 768], P(None, None, 'dp', 'tensor')
- qkv_bias_grad: float32 [2, 2, 2, 384], P(None, None, 'tensor', 'dp')
- out_weight_grad: float32 [2, 768, 768], P(None, 'tensor', 'dp')
- up_weight_grad: float32 [2, 768, 3072], P(None, 'dp', 'tensor')
- up_bias_grad: float32 [2, 2, 1536], P(None, 'tensor', 'dp')
- down_weight_grad: float32 [2, 3072, 768], P(None, 'tensor', 'dp')
- gain_grad: float32 [2, 2, 768], P(None, None, 'dp')
- shift_grad: float32 [2, 4, 768], P(None, None, 'dp')
Inputs may be any that keep to these rules, and one draw needn't show every extreme that they name: The 8 lengths of a row sum to 256; in every row the longest is exactly 64.
All inputs are finite; a program needn't handle non-finite values.
Results may differ from a plain program's by a relative error of at most 0.025.
Values may be sent and summed in bfloat16 or wider, within the bound.
No kernel may reach another device: no remote copies, remote signals or barrier semaphores. Data moves between devices by JAX's collectives and lax.ppermute only.
A program may use at most 192 MiB of HBM per device.

v0:
```python
import jax
import jax.numpy as jnp
from jax import lax
from jax.sharding import PartitionSpec as P

HD = 64
LEN = 256


SQRT_HALF = 0.7071067811865476
DENSITY_SCALE = 0.3989422804014327


def fetch_each(layer_weights):
    return (
        lax.all_gather(layer_weights[0], "dp", axis=1, tiled=True),
        lax.all_gather(layer_weights[1], "dp", axis=2, tiled=True),
        lax.all_gather(layer_weights[2], "dp", axis=1, tiled=True),
        lax.all_gather(layer_weights[3], "dp", axis=0, tiled=True),
        lax.all_gather(layer_weights[4], "dp", axis=1, tiled=True),
        lax.all_gather(layer_weights[5], "dp", axis=1, tiled=True),
        lax.all_gather(layer_weights[6], "dp", axis=1, tiled=True),
        lax.all_gather(layer_weights[7], "dp", axis=1, tiled=True),
    )


def gather_rows(half_rows):
    return lax.all_gather(half_rows, "tensor", axis=0, tiled=True)


def sum_rows(term_fn, row_count):
    return lax.psum_scatter(
        term_fn(jnp.int32(0), row_count * lax.axis_size("tensor")).astype(jnp.bfloat16),
        "tensor",
        scatter_dimension=0,
        tiled=True,
    ).astype(jnp.float32)


def segment_ids(row_lengths):
    finish = jnp.cumsum(row_lengths, dtype=jnp.int32)
    places = jnp.arange(LEN, dtype=jnp.int32)
    return jnp.sum((places[:, None] >= finish[None, :]).astype(jnp.int32), axis=1, dtype=jnp.int32)


def gelu_value(widened):
    return 0.5 * widened * (1.0 + lax.erf(widened * SQRT_HALF))


def gelu_slope(widened):
    return (
        0.5 * (1.0 + lax.erf(widened * SQRT_HALF))
        + widened * jnp.exp(-0.5 * widened * widened) * DENSITY_SCALE
    )


def norm_forward(summed, gain, shift):
    center = summed - jnp.mean(summed, axis=-1, keepdims=True)
    spread = jnp.mean(center * center, axis=-1, keepdims=True)
    scaling = lax.rsqrt(spread + 1e-12)
    normal = center * scaling
    return (normal * gain.astype(jnp.float32) + shift, normal, scaling)


def norm_backward(upstream, normal, scaling, gain):
    gain_part = jnp.sum(upstream * normal, axis=0)
    shift_part = jnp.sum(upstream, axis=0)
    scaled = upstream * gain.astype(jnp.float32)
    centered = scaled - jnp.mean(scaled, axis=-1, keepdims=True)
    back = scaling * (centered - normal * jnp.mean(scaled * normal, axis=-1, keepdims=True))
    return (back, gain_part, shift_part)


def split_heads(projected):
    length = projected.shape[0]
    heads = projected.shape[2] // HD
    block = min(length, 512)
    blocks = length // block
    keys_all = projected[:, 1].reshape(length, heads, HD)
    values_all = projected[:, 2].reshape(length, heads, HD)
    queries = projected[:, 0].reshape(blocks, block, heads, HD)
    return (length, heads, block, blocks, queries, keys_all, values_all)


def attention(projected, segment):
    length, heads, block, blocks, queries, keys_all, values_all = split_heads(projected)

    def one_block(packed):
        query_block, segment_block = packed
        raw_scores = (
            jnp.einsum("qhd,khd->hqk", query_block, keys_all, preferred_element_type=jnp.float32)
            * 0.125
        )
        allowed = segment_block[:, None] == segment[None, :]
        scores = jnp.where(allowed[None], raw_scores, -1000000000.0)
        highest = jnp.max(scores, axis=-1, keepdims=True)
        raised = jnp.exp(scores - highest)
        row_total = jnp.sum(raised, axis=-1, keepdims=True)
        weights = (raised / row_total).astype(jnp.bfloat16)
        context = jnp.einsum(
            "hqk,khd->qhd", weights, values_all, preferred_element_type=jnp.float32
        )
        return (
            context.reshape(block, heads * HD).astype(jnp.bfloat16),
            (highest + jnp.log(row_total))[:, :, 0],
        )

    context, log_totals = lax.map(one_block, (queries, segment.reshape(blocks, block)))
    return (context.reshape(length, heads * HD), log_totals)


def attention_back(projected, segment, log_totals, context_grad):
    length, heads, block, blocks, queries, keys_all, values_all = split_heads(projected)
    grad_blocks = context_grad.reshape(blocks, block, heads, HD)

    def one_block(carry, packed):
        key_grad, value_grad = carry
        query_block, segment_block, log_block, grad_block = packed
        raw_scores = (
            jnp.einsum("qhd,khd->hqk", query_block, keys_all, preferred_element_type=jnp.float32)
            * 0.125
        )
        allowed = segment_block[:, None] == segment[None, :]
        scores = jnp.where(allowed[None], raw_scores, -1000000000.0)
        weights = jnp.exp(scores - log_block[:, :, None])
        value_grad = value_grad + jnp.einsum(
            "hqk,qhd->khd",
            weights.astype(jnp.bfloat16),
            grad_block,
            preferred_element_type=jnp.float32,
        )
        weight_grad = jnp.einsum(
            "qhd,khd->hqk", grad_block, values_all, preferred_element_type=jnp.float32
        )
        inner = jnp.sum(weights * weight_grad, axis=-1, keepdims=True)
        score_grad = (weights * (weight_grad - inner)).astype(jnp.bfloat16)
        query_grad = (
            jnp.einsum("hqk,khd->qhd", score_grad, keys_all, preferred_element_type=jnp.float32)
            * 0.125
        )
        key_grad = (
            key_grad
            + jnp.einsum(
                "hqk,qhd->khd", score_grad, query_block, preferred_element_type=jnp.float32
            )
            * 0.125
        )
        return ((key_grad, value_grad), query_grad.reshape(block, heads * HD).astype(jnp.bfloat16))

    start_zero = jnp.zeros((length, heads, HD), jnp.float32)
    (key_grad, value_grad), query_grad = lax.scan(
        one_block,
        (start_zero, start_zero),
        (queries, segment.reshape(blocks, block), log_totals, grad_blocks),
    )
    return jnp.stack(
        [
            query_grad.reshape(length, heads * HD),
            key_grad.reshape(length, heads * HD).astype(jnp.bfloat16),
            value_grad.reshape(length, heads * HD).astype(jnp.bfloat16),
        ],
        axis=1,
    )


def forward_layer(x_half, segment, layer_weights):
    (
        layer_qkv,
        layer_qkv_bias,
        layer_out,
        layer_up,
        layer_up_bias,
        layer_down,
        layer_gains,
        layer_shifts,
    ) = layer_weights
    half_rows = x_half.shape[0]
    entering = gather_rows(x_half.astype(jnp.bfloat16))
    projected = jnp.einsum("td,kdc->tkc", entering, layer_qkv, preferred_element_type=jnp.float32)
    bias_rows = layer_qkv_bias.reshape(2, -1).astype(jnp.float32)
    bias_all = jnp.stack([bias_rows[0], jnp.zeros_like(bias_rows[0]), bias_rows[1]])
    projected = (projected + bias_all).astype(jnp.bfloat16)
    context, log_totals = attention(projected, segment)

    def out_term(first_row, row_count):
        return jnp.dot(context, layer_out, preferred_element_type=jnp.float32)

    shift_rows = layer_shifts.astype(jnp.float32)
    first_sum = x_half + sum_rows(out_term, half_rows) + shift_rows[0]
    normed, normal_one, scale_one = norm_forward(first_sum, layer_gains[0], shift_rows[1])
    widened_in = gather_rows(normed.astype(jnp.bfloat16))
    widened = jnp.dot(
        widened_in, layer_up, preferred_element_type=jnp.float32
    ) + layer_up_bias.reshape(-1).astype(jnp.float32)
    activated = gelu_value(widened).astype(jnp.bfloat16)

    def down_term(first_row, row_count):
        return jnp.dot(activated, layer_down, preferred_element_type=jnp.float32)

    second_sum = normed + sum_rows(down_term, half_rows) + shift_rows[2]
    result, normal_two, scale_two = norm_forward(second_sum, layer_gains[1], shift_rows[3])
    stored = (
        entering,
        projected,
        context,
        log_totals,
        normal_one,
        scale_one,
        widened_in,
        widened,
        activated,
        normal_two,
        scale_two,
    )
    return (result, stored)


def backward_layer(upstream, segment, layer_weights, stored):
    (
        layer_qkv,
        layer_qkv_bias,
        layer_out,
        layer_up,
        layer_up_bias,
        layer_down,
        layer_gains,
        layer_shifts,
    ) = layer_weights
    (
        entering,
        projected,
        context,
        log_totals,
        normal_one,
        scale_one,
        widened_in,
        widened,
        activated,
        normal_two,
        scale_two,
    ) = stored
    half_rows = upstream.shape[0]
    second_grad, gain_two, shift_two = norm_backward(
        upstream, normal_two, scale_two, layer_gains[1]
    )
    down_seed = gather_rows(second_grad.astype(jnp.bfloat16))
    down_grad = jnp.einsum("tf,td->fd", activated, down_seed, preferred_element_type=jnp.float32)
    active_grad = jnp.einsum("td,fd->tf", down_seed, layer_down, preferred_element_type=jnp.float32)
    widened_grad = (active_grad * gelu_slope(widened)).astype(jnp.bfloat16)
    up_grad = jnp.einsum("td,tf->df", widened_in, widened_grad, preferred_element_type=jnp.float32)
    up_bias_grad = jnp.sum(widened_grad, axis=0, dtype=jnp.float32).reshape(1, -1)

    def up_term(first_row, row_count):
        return jnp.einsum("tf,df->td", widened_grad, layer_up, preferred_element_type=jnp.float32)

    normed_grad = second_grad + sum_rows(up_term, half_rows)
    first_grad, gain_one, shift_one = norm_backward(
        normed_grad, normal_one, scale_one, layer_gains[0]
    )
    out_seed = gather_rows(first_grad.astype(jnp.bfloat16))
    out_grad = jnp.einsum("tc,td->cd", context, out_seed, preferred_element_type=jnp.float32)
    context_grad = jnp.einsum(
        "td,cd->tc", out_seed, layer_out, preferred_element_type=jnp.float32
    ).astype(jnp.bfloat16)
    projected_grad = attention_back(projected, segment, log_totals, context_grad)
    column_sums = jnp.sum(projected_grad, axis=0, dtype=jnp.float32)
    qkv_bias_grad = jnp.stack([column_sums[0], column_sums[2]]).reshape(2, 1, -1)
    qkv_grad = jnp.einsum(
        "td,tkc->kdc", entering, projected_grad, preferred_element_type=jnp.float32
    )

    def in_term(first_row, row_count):
        return jnp.einsum(
            "tkc,kdc->td", projected_grad, layer_qkv, preferred_element_type=jnp.float32
        )

    input_grad = first_grad + sum_rows(in_term, half_rows)
    gain_grads = jnp.stack([gain_one, gain_two])
    shift_grads = jnp.stack(
        [jnp.sum(first_grad, axis=0), shift_one, jnp.sum(second_grad, axis=0), shift_two]
    )
    return (
        input_grad,
        (
            qkv_grad,
            qkv_bias_grad,
            out_grad,
            up_grad,
            up_bias_grad,
            down_grad,
            gain_grads,
            shift_grads,
        ),
    )


def on_device(
    tokens,
    lengths,
    qkv_weight,
    qkv_bias,
    out_weight,
    up_weight,
    up_bias,
    down_weight,
    norm_gains,
    shifts,
    cotangent,
):
    params = (qkv_weight, qkv_bias, out_weight, up_weight, up_bias, down_weight, norm_gains, shifts)
    layers = qkv_weight.shape[0]
    micro = tokens.shape[0]

    def layer_params(layer_index):
        return fetch_each(tuple((member[layer_index] for member in params)))

    totals = [None] * layers
    out_list = []
    grad_list = []
    for micro_index in range(micro):
        segment = segment_ids(lengths[micro_index, 0])
        hidden = tokens[micro_index, 0].astype(jnp.float32)
        stored_list = []
        for layer_index in range(layers):
            hidden, stored = forward_layer(hidden, segment, layer_params(layer_index))
            stored_list.append(stored)
        out_list.append(hidden)
        upstream = cotangent[micro_index, 0].astype(jnp.float32)
        for layer_index in reversed(range(layers)):
            upstream, layer_grads = backward_layer(
                upstream, segment, layer_params(layer_index), stored_list[layer_index]
            )
            share_part = (
                lax.psum_scatter(layer_grads[0], "dp", scatter_dimension=1, tiled=True),
                lax.psum_scatter(layer_grads[1], "dp", scatter_dimension=2, tiled=True),
                lax.psum_scatter(layer_grads[2], "dp", scatter_dimension=1, tiled=True),
                lax.psum_scatter(layer_grads[3], "dp", scatter_dimension=0, tiled=True),
                lax.psum_scatter(layer_grads[4], "dp", scatter_dimension=1, tiled=True),
                lax.psum_scatter(layer_grads[5], "dp", scatter_dimension=1, tiled=True),
                lax.psum_scatter(layer_grads[6], "dp", scatter_dimension=1, tiled=True),
                lax.psum_scatter(layer_grads[7], "dp", scatter_dimension=1, tiled=True),
            )
            totals[layer_index] = (
                share_part
                if totals[layer_index] is None
                else jax.tree.map(jnp.add, totals[layer_index], share_part)
            )
        grad_list.append(upstream)
    stacked = [
        jnp.stack([layer_total[member_index] for layer_total in totals])
        for member_index in range(8)
    ]
    gain_total, shift_total = lax.psum((stacked[6], stacked[7]), "tensor")
    return (
        jnp.stack(out_list)[:, None],
        jnp.stack(grad_list)[:, None],
        stacked[0],
        stacked[1],
        stacked[2],
        stacked[3],
        stacked[4],
        stacked[5],
        gain_total,
        shift_total,
    )


def solution(mesh):
    in_specs = (
        P(None, "dp", "tensor", None),
        P(None, "dp", None),
        P(None, None, "dp", "tensor"),
        P(None, None, "tensor", "dp"),
        P(None, "tensor", "dp"),
        P(None, "dp", "tensor"),
        P(None, "tensor", "dp"),
        P(None, "tensor", "dp"),
        P(None, None, "dp"),
        P(None, None, "dp"),
        P(None, "dp", "tensor", None),
    )
    out_specs = (
        P(None, "dp", "tensor", None),
        P(None, "dp", "tensor", None),
        P(None, None, "dp", "tensor"),
        P(None, None, "tensor", "dp"),
        P(None, "tensor", "dp"),
        P(None, "dp", "tensor"),
        P(None, "tensor", "dp"),
        P(None, "tensor", "dp"),
        P(None, None, "dp"),
        P(None, None, "dp"),
    )
    return jax.shard_map(
        on_device, mesh=mesh, in_specs=in_specs, out_specs=out_specs, check_vma=False
    )
```

profile of v0, /device:TPU:12, one launch (start us, length us, event | category | flops | bytes accessed | tf_op | source)
XLA Modules:
  0.0 2628.3 jit_solution(13975036079830027915)
XLA Ops:
  10.9 32.0 %all-gather.2 = bf16[1,2,1,384]{2,1,0,3:T(2,128)(2,1)S(1)} all-gather(bf16[1,2,1,24]{2,1,0,3:T(2,128)(2,1)S(1)} %copy.360), channel_id=4, replica_groups=mesh['dp'=16,'tensor'=2] {'dp'}, dimensions={3}, use_global_device_ids=true | all-gather | bytes 1632 | tf_op jit(solution)/shard_map/all_gather | solution.py:17
  44.7 37.3 %all-gather.10 = bf16[1,2,1,384]{2,1,0,3:T(2,128)(2,1)S(1)} all-gather(bf16[1,2,1,24]{2,1,0,3:T(2,128)(2,1)S(1)} %copy.363), channel_id=12, replica_groups=mesh['dp'=16,'tensor'=2] {'dp'}, dimensions={3}, use_global_device_ids=true | all-gather | bytes 1632 | tf_op jit(solution)/shard_map/all_gather | solution.py:17
  90.8 41.1 %all-gather.3 = bf16[1,384,768]{1,2,0:T(8,128)(2,1)S(1)} all-gather(bf16[1,384,48]{1,2,0:T(8,128)(2,1)S(1)} %get-tuple-element.417), channel_id=5, replica_groups=mesh['dp'=16,'tensor'=2] {'dp'}, dimensions={2}, use_global_device_ids=true | all-gather | bytes 626688 | tf_op jit(solution)/shard_map/all_gather | solution.py:18
  155.2 37.8 %all-reduce.9 = (bf16[1536]{0:T(1024)(128)(2,1)S(1)}, bf16[1536]{0:T(1024)(128)(2,1)}) all-reduce(bf16[1536]{0:T(1024)(128)(2,1)S(1)} %dynamic-update-slice, bf16[1536]{0:T(1024)(128)(2,1)S(1)} %dynamic-update-slice.1), channel_id=9, replica_groups=mesh['dp'=16,'tensor'=2] {'dp'}, use_global_device_ids=true, to_apply=%add | all-reduce | flops 3072 | bytes 12288
  196.7 43.3 %all-gather.4 = bf16[1,4,768]{1,0,2:T(2,128)(2,1)S(1)} all-gather(bf16[1,4,48]{1,0,2:T(2,128)(2,1)} %copy.361), channel_id=6, replica_groups=mesh['dp'=16,'tensor'=2] {'dp'}, dimensions={2}, use_global_device_ids=true | all-gather | bytes 6528 | tf_op jit(solution)/shard_map/all_gather | solution.py:23
  240.4 38.3 %all-gather.5 = bf16[1,2,768]{1,0,2:T(2,128)(2,1)S(1)} all-gather(bf16[1,2,48]{1,0,2:T(2,128)(2,1)} %copy.362), channel_id=7, replica_groups=mesh['dp'=16,'tensor'=2] {'dp'}, dimensions={2}, use_global_device_ids=true | all-gather | bytes 3264 | tf_op jit(solution)/shard_map/all_gather | solution.py:22
  283.3 11.0 slice_reduce_fusion.4
  319.4 44.2 %all-gather.11 = bf16[1,384,768]{1,2,0:T(8,128)(2,1)} all-gather(bf16[1,384,48]{1,2,0:T(8,128)(2,1)} %get-tuple-element.416), channel_id=13, replica_groups=mesh['dp'=16,'tensor'=2] {'dp'}, dimensions={2}, use_global_device_ids=true | all-gather | bytes 626688 | tf_op jit(solution)/shard_map/all_gather | solution.py:18
  370.7 28.8 %all-gather.31.cloned.1.call-done = bf16[1,3,768,384]{3,2,1,0:T(8,128)(2,1)} async-done(((bf16[1,3,48,384]{3,2,1,0:T(8,128)(2,1)}), bf16[1,3,768,384]{3,2,1,0:T(8,128)(2,1)}) %all-gather.31.cloned.1.call-update) | async-done | bytes 1769488 | tf_op jit(solution)/shard_map/all_gather | solution.py:16
  432.7 32.2 %all-gather.12 = bf16[1,4,768]{1,0,2:T(2,128)(2,1)S(1)} all-gather(bf16[1,4,48]{1,0,2:T(2,128)(2,1)} %copy.364), channel_id=14, replica_groups=mesh['dp'=16,'tensor'=2] {'dp'}, dimensions={2}, use_global_device_ids=true | all-gather | bytes 6528 | tf_op jit(solution)/shard_map/all_gather | solution.py:23
  465.3 40.7 %all-gather.13 = bf16[1,2,768]{1,0,2:T(2,128)(2,1)S(1)} all-gather(bf16[1,2,48]{1,0,2:T(2,128)(2,1)} %copy.365), channel_id=15, replica_groups=mesh['dp'=16,'tensor'=2] {'dp'}, dimensions={2}, use_global_device_ids=true | all-gather | bytes 3264 | tf_op jit(solution)/shard_map/all_gather | solution.py:22
  510.6 11.8 slice_reduce_fusion
  531.6 39.8 %all-gather.35.cloned.1.call-done = bf16[1,1536,768]{1,2,0:T(8,128)(2,1)} async-done(((bf16[1,1536,48]{1,2,0:T(8,128)(2,1)}), bf16[1,1536,768]{1,2,0:T(8,128)(2,1)}) %all-gather.35.cloned.1.call-update) | async-done | bytes 2359312 | tf_op jit(solution)/shard_map/all_gather | solution.py:21
  585.2 8.2 reduce-scatter.49.cloned.1.call-done
  617.4 7.0 reduce-scatter.59.cloned.1.call-done
  778.0 6.3 copy.318
  788.8 6.4 copy.315
  818.2 27.3 %reduce-scatter.89.cloned.1.call-done = f32[96,1]{1,0:T(8,128)} async-done(((f32[1536,1]{1,0:T(8,128)}), f32[96,1]{1,0:T(8,128)}) %reduce-scatter.89.cloned.1.call-update) | async-done | bytes 400
  846.7 125.8 %reduce-scatter.93.cloned.1.call-done = f32[48,2]{1,0:T(8,128)} async-done(((f32[768,2]{1,0:T(8,128)}), f32[48,2]{1,0:T(8,128)}) %reduce-scatter.93.cloned.1.call-update) | async-done | bytes 400
  973.3 127.0 %reduce-scatter.87.cloned.1.call-done = f32[96,1]{1,0:T(8,128)} async-done(((f32[1536,1]{1,0:T(8,128)}), f32[96,1]{1,0:T(8,128)}) %reduce-scatter.87.cloned.1.call-update) | async-done | bytes 400
  1101.8 125.4 %reduce-scatter.97.cloned.1.call-done = f32[48,4]{1,0:T(8,128)} async-done(((f32[768,4]{1,0:T(8,128)}), f32[48,4]{1,0:T(8,128)}) %reduce-scatter.97.cloned.1.call-update) | async-done | bytes 784
  1228.2 30.6 %all-reduce.6 = (f32[2,1,384]{2,0,1:T(2,128)S(1)}, f32[2,1,384]{2,0,1:T(2,128)S(1)}) all-reduce(f32[2,1,384]{2,0,1:T(2,128)S(1)} %fusion.207, f32[2,1,384]{2,0,1:T(2,128)S(1)} %fusion.206), channel_id=55, replica_groups=mesh['dp'=16,'tensor'=2] {'dp'}, use_global_device_ids=true, to_apply=%region_73.74.clone | all-reduce | flops 1536 | bytes 12288
  1259.5 94.6 %reduce-scatter.91.cloned.1.call-done = f32[48,2]{1,0:T(8,128)} async-done(((f32[768,2]{1,0:T(8,128)}), f32[48,2]{1,0:T(8,128)}) %reduce-scatter.91.cloned.1.call-update) | async-done | bytes 400
  1354.9 126.0 %reduce-scatter.95.cloned.1.call-done = f32[48,4]{1,0:T(8,128)} async-done(((f32[768,4]{1,0:T(8,128)}), f32[48,4]{1,0:T(8,128)}) %reduce-scatter.95.cloned.1.call-update) | async-done | bytes 784
  1491.8 10.2 reduce-scatter.65.cloned.1.call-done
  1503.9 129.3 %reduce-scatter.77.cloned.1.call-done = f32[384,48]{0,1:T(8,128)} async-done(((f32[384,768]{0,1:T(8,128)}), f32[384,48]{0,1:T(8,128)}) %reduce-scatter.77.cloned.1.call-update) | async-done | bytes 73744 | tf_op jit(solution)/shard_map/reduce_scatter | solution.py:336
  1633.3 129.3 %reduce-scatter.75.cloned.1.call-done = f32[384,48]{0,1:T(8,128)} async-done(((f32[384,768]{0,1:T(8,128)}), f32[384,48]{0,1:T(8,128)}) %reduce-scatter.75.cloned.1.call-update) | async-done | bytes 73744 | tf_op jit(solution)/shard_map/reduce_scatter | solution.py:336
  1764.2 281.2 %all-reduce.12.cloned.1.call-done = (f32[3,768,384]{2,0,1:T(4,128)}, f32[3,768,384]{2,0,1:T(4,128)}) async-done(((f32[3,768,384]{2,0,1:T(4,128)}, f32[3,768,384]{2,0,1:T(4,128)}), (f32[3,768,384]{2,0,1:T(4,128)}, f32[3,768,384]{2,0,1:T(4,128)})) %all-reduce.12.cloned.1.call-update) | async-done | bytes 7077904
  2048.3 140.9 %reduce-scatter.81.cloned.1.call-done = f32[48,1536]{1,0:T(8,128)} async-done(((f32[768,1536]{1,0:T(8,128)}), f32[48,1536]{1,0:T(8,128)}) %reduce-scatter.81.cloned.1.call-update) | async-done | bytes 294928 | tf_op jit(solution)/shard_map/reduce_scatter | solution.py:337
  2189.2 143.4 %reduce-scatter.79.cloned.1.call-done = f32[48,1536]{1,0:T(8,128)} async-done(((f32[768,1536]{1,0:T(8,128)}), f32[48,1536]{1,0:T(8,128)}) %reduce-scatter.79.cloned.1.call-update) | async-done | bytes 294928 | tf_op jit(solution)/shard_map/reduce_scatter | solution.py:337
  2334.5 141.6 %reduce-scatter.85.cloned.1.call-done = f32[1536,48]{0,1:T(8,128)} async-done(((f32[1536,768]{0,1:T(8,128)}), f32[1536,48]{0,1:T(8,128)}) %reduce-scatter.85.cloned.1.call-update) | async-done | bytes 294928 | tf_op jit(solution)/shard_map/reduce_scatter | solution.py:339
  2476.1 143.3 %reduce-scatter.83.cloned.1.call-done = f32[1536,48]{0,1:T(8,128)} async-done(((f32[1536,768]{0,1:T(8,128)}), f32[1536,48]{0,1:T(8,128)}) %reduce-scatter.83.cloned.1.call-update) | async-done | bytes 294928 | tf_op jit(solution)/shard_map/reduce_scatter | solution.py:339
  (785 shorter events, 367.3 us)
Async XLA Ops:
  7.2 124.8 %all-gather.25.cloned.1.call-start = ((), (), s32[]{:S(2)}) async-start(), calls=%async_computation.44 | async-start | bytes 1880064 | tf_op jit(solution)/shard_map/all_gather | solution.py:16
  9.0 285.3 %reduce-scatter.43.cloned.1.call-start = ((), (), s32[]{:S(2)}) async-start(), calls=%async_computation.28 | async-start | bytes 589824 | tf_op jit(solution)/shard_map/reduce_scatter | solution.py:32
  142.2 153.7 %reduce-scatter.51.cloned.1.call-start = ((), (), s32[]{:S(2)}) async-start(), calls=%async_computation.32 | async-start | bytes 589824 | tf_op jit(solution)/shard_map/reduce_scatter | solution.py:32
  148.7 153.7 %all-gather.27.cloned.1.call-start = ((), (), s32[]{:S(2)}) async-start(), calls=%async_computation.45 | async-start | bytes 2506752 | tf_op jit(solution)/shard_map/all_gather | solution.py:19
  150.5 155.6 %all-gather.29.cloned.1.call-start = ((), (), s32[]{:S(2)}) async-start(), calls=%async_computation.46 | async-start | bytes 2506752 | tf_op jit(solution)/shard_map/all_gather | solution.py:21
  152.3 211.3 %reduce-scatter.53.cloned.1.call-start = ((), (), s32[]{:S(2)}) async-start(), calls=%async_computation.33 | async-start | bytes 589824 | tf_op jit(solution)/shard_map/reduce_scatter | solution.py:32
  309.9 53.7 %reduce-scatter.45.cloned.1.call-start = ((), (), s32[]{:S(2)}) async-start(), calls=%async_computation.29 | async-start | bytes 589824 | tf_op jit(solution)/shard_map/reduce_scatter | solution.py:32
  318.6 81.0 %all-gather.31.cloned.1.call-start = ((), (), s32[]{:S(2)}) async-start(), calls=%async_computation.47 | async-start | bytes 1880064 | tf_op jit(solution)/shard_map/all_gather | solution.py:16
  319.3 203.1 %reduce-scatter.47.cloned.1.call-start = ((), (), s32[]{:S(2)}) async-start(), calls=%async_computation.30 | async-start | bytes 589824 | tf_op jit(solution)/shard_map/reduce_scatter | solution.py:32
  418.9 103.5 %reduce-scatter.55.cloned.1.call-start = ((), (), s32[]{:S(2)}) async-start(), calls=%async_computation.34 | async-start | bytes 589824 | tf_op jit(solution)/shard_map/reduce_scatter | solution.py:32
  428.6 99.3 %all-gather.33.cloned.1.call-start = ((), (), s32[]{:S(2)}) async-start(), calls=%async_computation.48 | async-start | bytes 2506752 | tf_op jit(solution)/shard_map/all_gather | solution.py:19
  429.4 142.0 %all-gather.35.cloned.1.call-start = ((), (), s32[]{:S(2)}) async-start(), calls=%async_computation.49 | async-start | bytes 2506752 | tf_op jit(solution)/shard_map/all_gather | solution.py:21
  429.9 155.3 %reduce-scatter.57.cloned.1.call-start = ((), (), s32[]{:S(2)}) async-start(), calls=%async_computation.35 | async-start | bytes 589824 | tf_op jit(solution)/shard_map/reduce_scatter | solution.py:32
  583.8 30.5 %reduce-scatter.67.cloned.1.call-start = ((), (), s32[]{:S(2)}) async-start(), calls=%async_computation.40 | async-start | bytes 589824 | tf_op jit(solution)/shard_map/reduce_scatter | solution.py:32
  613.0 62.5 %reduce-scatter.69.cloned.1.call-start = ((), (), s32[]{:S(2)}) async-start(), calls=%async_computation.41 | async-start | bytes 589824 | tf_op jit(solution)/shard_map/reduce_scatter | solution.py:32
  675.5 60.8 %reduce-scatter.63.cloned.1.call-start = ((), (), s32[]{:S(2)}) async-start(), calls=%async_computation.38 | async-start | bytes 589824 | tf_op jit(solution)/shard_map/reduce_scatter | solution.py:32
  695.8 40.4 %reduce-scatter.71.cloned.1.call-start = ((), (), s32[]{:S(2)}) async-start(), calls=%async_computation.42 | async-start | bytes 589824 | tf_op jit(solution)/shard_map/reduce_scatter | solution.py:32
  704.7 140.9 %reduce-scatter.89.cloned.1.call-start = ((), (), s32[]{:S(2)}) async-start(), calls=%async_computation.57 | async-start | bytes 835584
  712.8 259.7 %reduce-scatter.93.cloned.1.call-start = ((), (), s32[]{:S(2)}) async-start(), calls=%async_computation.59 | async-start | bytes 417792
  722.2 378.1 %reduce-scatter.87.cloned.1.call-start = ((), (), s32[]{:S(2)}) async-start(), calls=%async_computation.56 | async-start | bytes 835584
  726.7 500.4 %reduce-scatter.97.cloned.1.call-start = ((), (), s32[]{:S(2)}) async-start(), calls=%async_computation.61 | async-start | bytes 417792
  736.1 618.0 %reduce-scatter.91.cloned.1.call-start = ((), (), s32[]{:S(2)}) async-start(), calls=%async_computation.58 | async-start | bytes 417792
  755.8 725.2 %reduce-scatter.95.cloned.1.call-start = ((), (), s32[]{:S(2)}) async-start(), calls=%async_computation.60 | async-start | bytes 417792
  758.2 732.6 %reduce-scatter.73.cloned.1.call-start = ((), (), s32[]{:S(2)}) async-start(), calls=%async_computation.43 | async-start | bytes 589824 | tf_op jit(solution)/shard_map/reduce_scatter | solution.py:32
  762.0 740.0 %reduce-scatter.65.cloned.1.call-start = ((), (), s32[]{:S(2)}) async-start(), calls=%async_computation.39 | async-start | bytes 589824 | tf_op jit(solution)/shard_map/reduce_scatter | solution.py:32
  768.4 864.8 %reduce-scatter.77.cloned.1.call-start = ((), (), s32[]{:S(2)}) async-start(), calls=%async_computation.51 | async-start | bytes 1253376 | tf_op jit(solution)/shard_map/reduce_scatter | solution.py:336
  770.9 991.7 %reduce-scatter.75.cloned.1.call-start = ((), (), s32[]{:S(2)}) async-start(), calls=%async_computation.50 | async-start | bytes 1253376 | tf_op jit(solution)/shard_map/reduce_scatter | solution.py:336
  773.4 1272.1 %all-reduce.12.cloned.1.call-start = ((), (), s32[]{:S(2)}) async-start(), calls=%async_computation.62 | async-start | bytes 18874368
  795.2 1394.0 %reduce-scatter.81.cloned.1.call-start = ((), (), s32[]{:S(2)}) async-start(), calls=%async_computation.53 | async-start | bytes 5013504 | tf_op jit(solution)/shard_map/reduce_scatter | solution.py:337
  800.3 1532.3 %reduce-scatter.79.cloned.1.call-start = ((), (), s32[]{:S(2)}) async-start(), calls=%async_computation.52 | async-start | bytes 5013504 | tf_op jit(solution)/shard_map/reduce_scatter | solution.py:337
  805.4 1670.7 %reduce-scatter.85.cloned.1.call-start = ((), (), s32[]{:S(2)}) async-start(), calls=%async_computation.55 | async-start | bytes 5013504 | tf_op jit(solution)/shard_map/reduce_scatter | solution.py:339
  810.6 1808.9 %reduce-scatter.83.cloned.1.call-start = ((), (), s32[]{:S(2)}) async-start(), calls=%async_computation.54 | async-start | bytes 5013504 | tf_op jit(solution)/shard_map/reduce_scatter | solution.py:339
  (199 other events, 4980.2 us)
Sparse Core Ops, SparseCore 0:
  11.3 60.2 all-gather.24
  142.4 13.8 reduce-scatter.42
  159.0 9.0 reduce-scatter.50
  171.4 65.7 all-gather.26
  240.4 61.5 all-gather.28
  310.0 15.6 reduce-scatter.52
  328.5 8.9 reduce-scatter.44
  340.2 59.2 all-gather.30
  429.1 8.9 reduce-scatter.54
  441.5 66.1 all-gather.32
  510.3 60.9 all-gather.34
  584.5 8.8 reduce-scatter.48
  604.4 8.9 reduce-scatter.66
  615.5 8.9 reduce-scatter.58
  662.4 8.9 reduce-scatter.68
  675.6 8.9 reduce-scatter.60
  696.0 8.9 reduce-scatter.62
  707.0 8.9 reduce-scatter.70
  720.7 124.8 reduce-scatter.88
  850.2 122.2 reduce-scatter.92
  977.2 123.0 reduce-scatter.86
  1104.8 122.2 reduce-scatter.96
  1231.8 122.2 reduce-scatter.90
  1358.6 122.2 reduce-scatter.94
  1493.1 8.9 reduce-scatter.64
  1506.8 126.4 reduce-scatter.76
  1637.9 124.6 reduce-scatter.74
  1768.9 276.4 all-reduce.11
  2050.6 138.5 reduce-scatter.80
  2194.2 138.3 reduce-scatter.78
  2337.8 138.2 reduce-scatter.84
  2481.3 138.1 reduce-scatter.82
  (3 shorter events, 20.9 us)
where the time goes:
time: 2640 us; the launch traced here: 2630 us
  waiting for transfers between devices  1840 us (70%)
  blocking collectives  416 us (16%)
  local copies, waits for them, and re-layouts  141 us (5%)
  matrix products  127 us (5%)
  other arithmetic  79.9 us (3%)
    unnamed x42, waiting for transfers between devices  910 us
    reduce_scatter x2, waiting for transfers between devices, on_device(): lax.psum_scatter(layer_grads[5], 'dp', scatter_dimension=1, tiled=True)  285 us
    reduce_scatter x2, waiting for transfers between devices, on_device(): lax.psum_scatter(layer_grads[3], 'dp', scatter_dimension=0, tiled=True)  284 us
    reduce_scatter x2, waiting for transfers between devices, on_device(): lax.psum_scatter(layer_grads[2], 'dp', scatter_dimension=1, tiled=True)  259 us
    all_gather x2, blocking collectives, fetch_each(): lax.all_gather(layer_weights[2], 'dp', axis=1, tiled=True)  85.3 us
    all_gather x2, blocking collectives, fetch_each(): lax.all_gather(layer_weights[6], 'dp', axis=1, tiled=True)  79 us
    all_gather x2, blocking collectives, fetch_each(): lax.all_gather(layer_weights[7], 'dp', axis=1, tiled=True)  75.4 us
    all_gather x2, blocking collectives, fetch_each(): lax.all_gather(layer_weights[1], 'dp', axis=2, tiled=True)  69.3 us
  transfers between devices with their start and end apart: 35, of which 20 were waited for; matrix products, arithmetic and copies ran while one was open for 9% of the time, Pallas kernels for 0%

commit v1 on v0

v1 whole, which is shorter than its diff:
```python
import jax
import jax.numpy as jnp
from jax import lax
from jax.sharding import PartitionSpec as P

HD = 64
SQRT_HALF = 0.7071067811865476
DENSITY_SCALE = 0.3989422804014327
F32 = jnp.float32
BF16 = jnp.bfloat16
SMALL = 128


def dp_coords():
    index = lax.axis_index("dp")
    return index // 4, (index // 2) % 2, index % 2


def swap(value, bit):
    return lax.ppermute(value, "dp", [(i, i ^ bit) for i in range(16)])


def z_move(value, step, lines):
    return lax.ppermute(
        value, "dp", [(4 * i + j, 4 * (i + step) + j) for i in lines for j in range(4)]
    )


def other_core(value):
    return lax.ppermute(value, "tensor", [(0, 1), (1, 0)])


def ordered(bit, mine, theirs):
    return jnp.stack([jnp.where(bit == 0, mine, theirs), jnp.where(bit == 0, theirs, mine)])


def z_gather(own, z):
    right, left = [own], [own]
    for k in range(3):
        right.append(z_move(right[-1], 1, range(k, 3)))
        left.append(z_move(left[-1], -1, range(3 - k, 0, -1)))
    around = [own] + [jnp.where(z >= k, right[k], left[4 - k]) for k in (1, 2, 3)]
    placed = []
    for source in range(4):
        chosen = around[0]
        for k in (1, 2, 3):
            chosen = jnp.where((z - source) % 4 == k, around[k], chosen)
        placed.append(chosen)
    return jnp.stack(placed)


def gather_grid(shard):
    z, y, x = dp_coords()
    rows = shard.shape[0] // 3
    first, rest = shard[:rows], shard[rows:]
    a_x = ordered(x, first, swap(first, 1))
    a_yx = ordered(y, a_x, swap(a_x, 2))
    lines = z_gather(rest, z)
    a = z_gather(a_yx, z)
    b, c = lines[:, :rows], lines[:, rows:]
    b_x = ordered(x, b, swap(b, 1))
    b_yx = ordered(y, b_x, swap(b_x, 2))
    c_y = ordered(y, c, swap(c, 2))
    c_xy = ordered(x, c_y, swap(c_y, 1))
    whole = jnp.stack([a, b_yx.transpose(2, 0, 1, 3, 4), c_xy.transpose(2, 1, 0, 3, 4)], axis=3)
    return whole.reshape(16 * shard.shape[0], shard.shape[1])


def z_reduce(parts, z):
    def chunk(k):
        return lax.dynamic_index_in_dim(parts, jnp.clip(k, 0, 3), 0, keepdims=False)

    r_in = l_in = None
    for s in (1, 2, 3):
        send_r, send_l = chunk(z + 4 - s), chunk(z - 4 + s)
        if s > 1:
            send_r = (send_r.astype(F32) + jnp.where(z > 0, r_in.astype(F32), 0.0)).astype(BF16)
            send_l = (send_l.astype(F32) + jnp.where(z < 3, l_in.astype(F32), 0.0)).astype(BF16)
        r_in = z_move(send_r, 1, range(0, s))
        l_in = z_move(send_l, -1, range(3, 3 - s, -1))
    return chunk(z).astype(F32) + r_in.astype(F32) + l_in.astype(F32)


def swap_reduce(parts, bit, place, dim):
    theirs = lax.dynamic_index_in_dim(parts, 1 - place, dim, keepdims=False).astype(BF16)
    mine = lax.dynamic_index_in_dim(parts, place, dim, keepdims=False).astype(F32)
    return mine + swap(theirs, bit).astype(F32)


def reduce_grid(partial):
    z, y, x = dp_coords()
    rows, columns = partial.shape[0] // 48, partial.shape[1]
    grid = partial.reshape(4, 2, 2, 3, rows, columns)
    a, b, c = grid[:, :, :, 0], grid[:, :, :, 1], grid[:, :, :, 2]
    b = swap_reduce(swap_reduce(b, 2, y, 1), 1, x, 1).astype(BF16)
    c = swap_reduce(swap_reduce(c, 1, x, 2), 2, y, 1).astype(BF16)
    a = z_reduce(a, z)
    rest = z_reduce(jnp.concatenate([b, c], 1), z)
    a = swap_reduce(swap_reduce(a, 1, x, 1), 2, y, 0)
    return jnp.concatenate([a, rest], 0)


def gather_dp(shard):
    if lax.axis_size("dp") == 16:
        return gather_grid(shard)
    return lax.all_gather(shard, "dp", axis=0, tiled=True)


def reduce_dp(partial):
    if lax.axis_size("dp") == 16:
        return reduce_grid(partial)
    return lax.psum_scatter(partial.astype(F32), "dp", scatter_dimension=0, tiled=True)


def segment_ids(row_lengths, length):
    finish = jnp.cumsum(row_lengths, dtype=jnp.int32)
    places = jnp.arange(length, dtype=jnp.int32)
    return jnp.sum((places[:, None] >= finish[None, :]).astype(jnp.int32), axis=1, dtype=jnp.int32)


def norm_forward(summed, gain, shift):
    center = summed - jnp.mean(summed, axis=-1, keepdims=True)
    spread = jnp.mean(center * center, axis=-1, keepdims=True)
    scaling = lax.rsqrt(spread + 1e-12)
    normal = center * scaling
    return (normal * gain + shift, normal, scaling)


def norm_backward(upstream, normal, scaling, gain):
    gain_part = jnp.sum(upstream * normal, axis=0)
    shift_part = jnp.sum(upstream, axis=0)
    scaled = upstream * gain
    centered = scaled - jnp.mean(scaled, axis=-1, keepdims=True)
    back = scaling * (centered - normal * jnp.mean(scaled * normal, axis=-1, keepdims=True))
    return (back, gain_part, shift_part)


def nn(a, b):
    return jnp.dot(a, b, preferred_element_type=F32)


def nt(a, b):
    return lax.dot_general(a, b, (((1,), (1,)), ((), ())), preferred_element_type=F32)


def tn(a, b):
    return lax.dot_general(a, b, (((0,), (0,)), ((), ())), preferred_element_type=F32)


def heads_of(part, heads):
    return part.reshape(part.shape[0], heads, HD).transpose(1, 0, 2)


def attention(q, k, v, allowed):
    heads = q.shape[1] // HD
    q, k, v = (heads_of(t, heads) for t in (q, k, v))
    scores = jnp.einsum("hqd,hkd->hqk", q, k, preferred_element_type=F32) * 0.125
    scores = jnp.where(allowed[None], scores, -1000000000.0)
    highest = jnp.max(scores, axis=-1, keepdims=True)
    raised = jnp.exp(scores - highest)
    total = jnp.sum(raised, axis=-1, keepdims=True)
    weights = (raised / total).astype(BF16)
    context = jnp.einsum("hqk,hkd->hqd", weights, v, preferred_element_type=F32).astype(BF16)
    return context.transpose(1, 0, 2).reshape(q.shape[1], heads * HD), highest + jnp.log(total)


def attention_back(q, k, v, allowed, log_totals, context_grad):
    heads = q.shape[1] // HD
    length = q.shape[0]
    q, k, v, g = (heads_of(t, heads) for t in (q, k, v, context_grad))
    scores = jnp.einsum("hqd,hkd->hqk", q, k, preferred_element_type=F32) * 0.125
    scores = jnp.where(allowed[None], scores, -1000000000.0)
    weights = jnp.exp(scores - log_totals)
    dv = jnp.einsum("hqk,hqd->hkd", weights.astype(BF16), g, preferred_element_type=F32)
    dw = jnp.einsum("hqd,hkd->hqk", g, v, preferred_element_type=F32)
    inner = jnp.sum(weights * dw, axis=-1, keepdims=True)
    ds = (weights * (dw - inner)).astype(BF16)
    dq = jnp.einsum("hqk,hkd->hqd", ds, k, preferred_element_type=F32) * 0.125
    dk = jnp.einsum("hqk,hqd->hkd", ds, q, preferred_element_type=F32) * 0.125
    return [t.astype(BF16).transpose(1, 0, 2).reshape(length, heads * HD) for t in (dq, dk, dv)]


class Sizes:
    def __init__(self, qkv, out, up):
        self.part = qkv.shape[3]
        self.hidden = up.shape[2]
        p = self.part
        self.qkv = slice(0, 3 * p)
        self.out = slice(3 * p, 4 * p)
        self.up = slice(4 * p, 4 * p + self.hidden)
        self.down = slice(4 * p + self.hidden, 4 * p + 2 * self.hidden)
        self.small = slice(4 * p + 2 * self.hidden, 4 * p + 2 * self.hidden + SMALL)


def pack(qkv, qkv_bias, out, up, up_bias, down, gains, shifts):
    rows = qkv.shape[1]
    small = jnp.concatenate(
        [
            gains.T,
            shifts.T,
            qkv_bias.reshape(rows, -1),
            up_bias.reshape(-1, rows).T,
        ],
        axis=1,
    )
    small = jnp.pad(small, ((0, 0), (0, SMALL - small.shape[1])))
    return jnp.concatenate(
        [qkv.transpose(1, 0, 2).reshape(rows, -1), out.T, up, down.T, small], axis=1
    )


def unpack_small(small, rows):
    shards = small.shape[0] // rows
    values = small.astype(F32)
    gains, shifts = values[:, :2].T, values[:, 2:6].T
    qkv_bias = values[:, 6].reshape(shards, 2, rows // 2).transpose(1, 0, 2).reshape(2, -1)
    up_bias = values[:, 7:9].reshape(shards, rows, 2).transpose(0, 2, 1).reshape(-1)
    return gains, shifts, qkv_bias, up_bias


def pack_small_grads(gains, shifts, qkv_bias, up_bias, rows):
    shards = gains.shape[1] // rows
    columns = [
        gains.T,
        shifts.T,
        qkv_bias.reshape(2, shards, rows // 2).transpose(1, 0, 2).reshape(-1, 1),
        up_bias.reshape(shards, 2, rows).transpose(0, 2, 1).reshape(-1, 2),
    ]
    small = jnp.concatenate(columns, axis=1)
    return jnp.pad(small, ((0, 0), (0, SMALL - small.shape[1])))


def forward_layer(x, allowed, mine, theirs, smalls, sizes):
    gains, shifts, qb_m, ub_m, qb_t, ub_t = smalls
    p = sizes.part
    entering = x.astype(BF16)
    zero = jnp.zeros((p,), F32)

    def project(weights, qb):
        bias = jnp.concatenate([qb[0], zero, qb[1]])
        return (nn(entering, weights[:, sizes.qkv]) + bias).astype(BF16)

    proj_m, proj_t = project(mine, qb_m), project(theirs, qb_t)
    ctx_m, log_m = attention(proj_m[:, :p], proj_m[:, p : 2 * p], proj_m[:, 2 * p :], allowed)
    ctx_t, log_t = attention(proj_t[:, :p], proj_t[:, p : 2 * p], proj_t[:, 2 * p :], allowed)
    first_sum = x + nt(ctx_m, mine[:, sizes.out]) + nt(ctx_t, theirs[:, sizes.out]) + shifts[0]
    normed, normal_one, scale_one = norm_forward(first_sum, gains[0], shifts[1])
    widened_in = normed.astype(BF16)
    wide_m = nn(widened_in, mine[:, sizes.up]) + ub_m
    wide_t = nn(widened_in, theirs[:, sizes.up]) + ub_t

    def gelu(w):
        return (0.5 * w * (1.0 + lax.erf(w * SQRT_HALF))).astype(BF16)

    act_m, act_t = gelu(wide_m), gelu(wide_t)
    second_sum = (
        normed + nt(act_m, mine[:, sizes.down]) + nt(act_t, theirs[:, sizes.down]) + shifts[2]
    )
    result, normal_two, scale_two = norm_forward(second_sum, gains[1], shifts[3])
    both = dict(
        entering=jnp.concatenate([entering, other_core(entering)]),
        ctx=jnp.concatenate([ctx_m, other_core(ctx_t)]),
        widened_in=jnp.concatenate([widened_in, other_core(widened_in)]),
        act=jnp.concatenate([act_m, other_core(act_t)]),
    )
    stored = (
        proj_m,
        proj_t,
        log_m,
        log_t,
        normal_one,
        scale_one,
        wide_m,
        wide_t,
        normal_two,
        scale_two,
        both,
    )
    return result, stored


def backward_layer(upstream, allowed, mine, theirs, smalls, stored, sizes):
    gains = smalls[0]
    proj_m, proj_t, log_m, log_t, normal_one, scale_one, wide_m, wide_t, normal_two, scale_two, both = stored
    p = sizes.part
    second_grad, gain_two, shift_two = norm_backward(upstream, normal_two, scale_two, gains[1])
    down_seed = second_grad.astype(BF16)

    def slope(w):
        return (
            0.5 * (1.0 + lax.erf(w * SQRT_HALF)) + w * jnp.exp(-0.5 * w * w) * DENSITY_SCALE
        )

    wg_m = (nn(down_seed, mine[:, sizes.down]) * slope(wide_m)).astype(BF16)
    wg_t = (nn(down_seed, theirs[:, sizes.down]) * slope(wide_t)).astype(BF16)
    seeds = jnp.concatenate([down_seed, other_core(down_seed)])
    down_grad = tn(seeds, both["act"])
    wg_both = jnp.concatenate([wg_m, other_core(wg_t)])
    up_grad = tn(both["widened_in"], wg_both)
    up_bias_grad = jnp.sum(wg_both.astype(F32), axis=0)
    normed_grad = second_grad + nt(wg_m, mine[:, sizes.up]) + nt(wg_t, theirs[:, sizes.up])
    first_grad, gain_one, shift_one = norm_backward(normed_grad, normal_one, scale_one, gains[0])
    out_seed = first_grad.astype(BF16)
    seeds = jnp.concatenate([out_seed, other_core(out_seed)])
    out_grad = tn(seeds, both["ctx"])
    cg_m = nn(out_seed, mine[:, sizes.out]).astype(BF16)
    cg_t = nn(out_seed, theirs[:, sizes.out]).astype(BF16)
    pg_m = attention_back(
        proj_m[:, :p], proj_m[:, p : 2 * p], proj_m[:, 2 * p :], allowed, log_m, cg_m
    )
    pg_t = attention_back(
        proj_t[:, :p], proj_t[:, p : 2 * p], proj_t[:, 2 * p :], allowed, log_t, cg_t
    )
    pg_m, pg_t = jnp.concatenate(pg_m, axis=1), jnp.concatenate(pg_t, axis=1)
    pg_both = jnp.concatenate([pg_m, other_core(pg_t)])
    qkv_grad = tn(both["entering"], pg_both)
    column_sums = jnp.sum(pg_both.astype(F32), axis=0)
    qkv_bias_grad = jnp.stack([column_sums[:p], column_sums[2 * p :]])
    input_grad = first_grad + nt(pg_m, mine[:, sizes.qkv]) + nt(pg_t, theirs[:, sizes.qkv])
    norms = jnp.stack(
        [gain_one, gain_two, jnp.sum(first_grad, axis=0), shift_one, jnp.sum(second_grad, axis=0), shift_two]
    )
    norms = norms + other_core(norms)
    return input_grad, (qkv_grad, out_grad, up_grad, down_grad, norms, qkv_bias_grad, up_bias_grad)


def on_device(
    tokens,
    lengths,
    qkv_weight,
    qkv_bias,
    out_weight,
    up_weight,
    up_bias,
    down_weight,
    norm_gains,
    shifts,
    cotangent,
):
    layers = qkv_weight.shape[0]
    micro, half = tokens.shape[0], tokens.shape[2]
    assert micro == 2 and lax.axis_size("tensor") == 2 and tokens.shape[1] == 1
    length = 2 * half
    core = lax.axis_index("tensor")
    sizes = Sizes(qkv_weight, out_weight, up_weight)
    rows = qkv_weight.shape[2]

    def whole_row(values):
        kept = lax.dynamic_index_in_dim(values[:, 0], core, 0, keepdims=False)
        given = lax.dynamic_index_in_dim(values[:, 0], 1 - core, 0, keepdims=False)
        return jnp.concatenate([kept, other_core(given)], axis=0).astype(F32)

    def split_row(row):
        kept, given = row[:half], row[half:]
        back = other_core(given)
        return jnp.stack([jnp.where(core == 0, kept, back), jnp.where(core == 0, back, kept)])[:, None]

    segment = segment_ids(lax.dynamic_index_in_dim(lengths[:, 0], core, 0, keepdims=False), length)
    segment = jnp.where(core == 0, segment, jnp.roll(segment, half))
    allowed = segment[:, None] == segment[None, :]

    weights, smalls = [], []
    params = (qkv_weight, qkv_bias, out_weight, up_weight, up_bias, down_weight, norm_gains, shifts)
    for layer in range(layers):
        shard = pack(*(member[layer] for member in params))
        mine = gather_dp(shard)
        theirs = other_core(mine)
        gains, shift_rows, qb_m, ub_m = unpack_small(mine[:, sizes.small], rows)
        _, _, qb_t, ub_t = unpack_small(theirs[:, sizes.small], rows)
        weights.append((mine, theirs))
        smalls.append((gains, shift_rows, qb_m, ub_m, qb_t, ub_t))

    hidden = whole_row(tokens)
    stored = []
    for layer in range(layers):
        hidden, kept = forward_layer(hidden, allowed, *weights[layer], smalls[layer], sizes)
        stored.append(kept)
    out_tokens = split_row(hidden)
    upstream = whole_row(cotangent)
    grads = [None] * layers
    for layer in reversed(range(layers)):
        upstream, found = backward_layer(
            upstream, allowed, *weights[layer], smalls[layer], stored[layer], sizes
        )
        qkv_grad, out_grad, up_grad, down_grad, norms, qkv_bias_grad, up_bias_grad = found
        small = pack_small_grads(norms[:2], norms[2:], qkv_bias_grad, up_bias_grad, rows)
        partial = jnp.concatenate([qkv_grad, out_grad, up_grad, down_grad, small], axis=1).astype(BF16)
        total = reduce_dp(partial)
        small = total[:, sizes.small]
        grads[layer] = (
            total[:, sizes.qkv].reshape(rows, 3, -1).transpose(1, 0, 2),
            small[:, 6].reshape(2, 1, -1),
            total[:, sizes.out].T,
            total[:, sizes.up],
            small[:, 7:9].T.reshape(1, -1),
            total[:, sizes.down].T,
            small[:, :2].T,
            small[:, 2:6].T,
        )
    token_grad = split_row(upstream)
    stacked = [jnp.stack([grads[layer][i] for layer in range(layers)]) for i in range(8)]
    return (out_tokens, token_grad, *stacked)


def solution(mesh):
    in_specs = (
        P(None, "dp", "tensor", None),
        P(None, "dp", None),
        P(None, None, "dp", "tensor"),
        P(None, None, "tensor", "dp"),
        P(None, "tensor", "dp"),
        P(None, "dp", "tensor"),
        P(None, "tensor", "dp"),
        P(None, "tensor", "dp"),
        P(None, None, "dp"),
        P(None, None, "dp"),
        P(None, "dp", "tensor", None),
    )
    out_specs = (
        P(None, "dp", "tensor", None),
        P(None, "dp", "tensor", None),
        P(None, None, "dp", "tensor"),
        P(None, None, "tensor", "dp"),
        P(None, "tensor", "dp"),
        P(None, "dp", "tensor"),
        P(None, "tensor", "dp"),
        P(None, "tensor", "dp"),
        P(None, None, "dp"),
        P(None, None, "dp"),
    )
    return jax.shard_map(
        on_device, mesh=mesh, in_specs=in_specs, out_specs=out_specs, check_vma=False
    )
```

time: 2640 us -> 612 us (0.23)
  waiting for transfers between devices: 1840 us -> 177 us
  blocking collectives: 416 us -> 0 us
  starting transfers between devices: 1.7 us -> 152 us
  local copies, waits for them, and re-layouts: 141 us -> 78.3 us
    unnamed x42 -> x0, waiting for transfers between devices: 910 us -> none
    reduce_scatter x22 -> x0, waiting for transfers between devices: 865 us -> none  [the longest x2 285 us: on_device(): lax.psum_scatter(layer_grads[5], 'dp', scatter_dimension=1, tiled=True)]
    all_gather x24 -> x0, blocking collectives: 344 us -> none  [the longest x2 85.3 us: fetch_each(): lax.all_gather(layer_weights[2], 'dp', axis=1, tiled=True)]
    ppermute x0 -> x96, waiting for transfers between devices: none -> 177 us  [the longest x48 111 us: z_move(): lax.ppermute(value, 'dp', [(4 * i + j, 4 * (i + step) + j) for i in lines...]
    ppermute x0 -> x96, starting transfers between devices: none -> 152 us  [the longest x48 122 us: z_move(): lax.ppermute(value, 'dp', [(4 * i + j, 4 * (i + step) + j) for i in lines...]
    all_gather x6 -> x0, waiting for transfers between devices: 68.7 us -> none  [the longest x2 39.8 us: fetch_each(): lax.all_gather(layer_weights[5], 'dp', axis=1, tiled=True)]
    unnamed x2 -> x0, blocking collectives: 68.3 us -> none
    dot_general x72 -> x64, matrix products: 127 us -> 133 us  [the longest x16 45.5 us: nn(): return jnp.dot(a, b, preferred_element_type=F32)]
  transfers between devices with their start and end apart: 35 -> 96, of which waited for: 20 -> 30; matrix products, arithmetic and copies ran while one was open for 9% -> 29% of each run, Pallas kernels for 0% -> 0%
where the time goes in v1:
time: 612 us; the launch traced here: 600 us
  waiting for transfers between devices  177 us (29%)
  starting transfers between devices  152 us (25%)
  matrix products  133 us (22%)
  local copies, waits for them, and re-layouts  78.3 us (13%)
  other arithmetic  55.7 us (9%)
    ppermute x48, starting transfers between devices, z_move(): lax.ppermute(value, 'dp', [(4 * i + j, 4 * (i + step) + j) for i in lines...  122 us
    ppermute x48, waiting for transfers between devices, z_move(): lax.ppermute(value, 'dp', [(4 * i + j, 4 * (i + step) + j) for i in lines...  111 us
    ppermute x24, waiting for transfers between devices, swap(): return lax.ppermute(value, 'dp', [(i, i ^ bit) for i in range(16)])  55.8 us
    dot_general x16, matrix products, nn(): return jnp.dot(a, b, preferred_element_type=F32)  45.5 us
    dot_general x16, matrix products, nt(): lax.dot_general(a, b, (((1,), (1,)), ((), ())), preferred_element_type=F32)  40 us
    unnamed x312, local copies, waits for them, and re-layouts  25.1 us
    ppermute x24, starting transfers between devices, swap(): return lax.ppermute(value, 'dp', [(i, i ^ bit) for i in range(16)])  23.5 us
    dot_general x8, matrix products, tn(): lax.dot_general(a, b, (((0,), (0,)), ((), ())), preferred_element_type=F32)  23.2 us
  transfers between devices with their start and end apart: 96, of which 30 were waited for; matrix products, arithmetic and copies ran while one was open for 29% of the time, Pallas kernels for 0%

profile of v1, /device:TPU:12, one launch (start us, length us, event | category | flops | bytes accessed | tf_op | source)
XLA Modules:
  0.0 600.4 jit_solution(93671394190619913)
XLA Ops:
  20.3 4.6 collective-permute-done.20
  32.5 4.0 collective-permute-start.29
  38.6 3.9 collective-permute-start.3
  47.3 3.9 collective-permute-start.22
  52.8 4.4 collective-permute-start.33
  58.4 10.8 %collective-permute-done.33 = bf16[32,4736]{1,0:T(8,128)(2,1)S(1)} collective-permute-done((bf16[32,4736]{1,0:T(8,128)(2,1)S(1)}, bf16[32,4736]{1,0:T(8,128)(2,1)S(1)}, u32[]{:S(2)}, u32[]{:S(2)}) %collective-permute-start.33) | collective-permute-done | bytes 303136 | tf_op jit(solution)/shard_map/ppermute | solution.py:24
  70.4 4.4 collective-permute-start.25
  75.4 7.7 %collective-permute-done.17 = bf16[4,16,4736]{2,1,0:T(8,128)(2,1)S(1)} collective-permute-done((bf16[4,16,4736]{2,1,0:T(8,128)(2,1)S(1)}, bf16[4,16,4736]{2,1,0:T(8,128)(2,1)S(1)}, u32[]{:S(2)}, u32[]{:S(2)}) %collective-permute-start.17) | collective-permute-done | bytes 606240 | tf_op jit(solution)/shard_map/ppermute | solution.py:20
  84.0 15.1 %collective-permute-start.4 = (bf16[2,2,16,4736]{3,2,1,0:T(8,128)(2,1)S(1)}, bf16[2,2,16,4736]{3,2,1,0:T(8,128)(2,1)S(1)}, u32[]{:S(2)}, u32[]{:S(2)}) collective-permute-start(bf16[2,2,16,4736]{3,2,1,0:T(8,128)(2,1)S(1)} %collective-permute-done.3), channel_id=1, source_target_pairs={{8,16},{10,18},{12,20},{14,22},{16,24},{18,26},{20,28},{22,30},{9,... | collective-permute-start | bytes 1818632 | tf_op jit(solution)/shard_map/ppermute | solution.py:24
  101.1 4.0 collective-permute-start.23
  109.0 4.2 collective-permute-done.4
  121.4 6.7 %collective-permute-done.26 = bf16[2,2,16,4736]{3,2,1,0:T(8,128)(2,1)S(1)} collective-permute-done((bf16[2,2,16,4736]{3,2,1,0:T(8,128)(2,1)S(1)}, bf16[2,2,16,4736]{3,2,1,0:T(8,128)(2,1)S(1)}, u32[]{:S(2)}, u32[]{:S(2)}) %collective-permute-start.26) | collective-permute-done | bytes 606240 | tf_op jit(solution)/shard_map/ppermute | solution.py:24
  130.3 6.2 %collective-permute-done.8 = bf16[2,2,16,4736]{3,2,1,0:T(8,128)(2,1)S(1)} collective-permute-done((bf16[2,2,16,4736]{3,2,1,0:T(8,128)(2,1)S(1)}, bf16[2,2,16,4736]{3,2,1,0:T(8,128)(2,1)S(1)}, u32[]{:S(2)}, u32[]{:S(2)}) %collective-permute-start.8) | collective-permute-done | bytes 606240 | tf_op jit(solution)/shard_map/ppermute | solution.py:24
  136.5 4.4 collective-permute-start.27
  143.5 4.9 collective-permute-done.27
  155.9 12.0 %collective-permute-done.37 = bf16[2,4,16,4736]{3,2,1,0:T(8,128)(2,1)S(1)} collective-permute-done((bf16[2,4,16,4736]{3,2,1,0:T(8,128)(2,1)S(1)}, bf16[2,4,16,4736]{3,2,1,0:T(8,128)(2,1)S(1)}, u32[]{:S(2)}, u32[]{:S(2)}) %collective-permute-start.37) | collective-permute-done | bytes 1212448 | tf_op jit(solution)/shard_map/ppermute | solution.py:20
  174.7 10.3 %collective-permute-done = bf16[128,768]{1,0:T(8,128)(2,1)S(1)} collective-permute-done((bf16[128,768]{1,0:T(8,128)(2,1)S(1)}, bf16[128,768]{1,0:T(8,128)(2,1)S(1)}, u32[]{:S(2)}, u32[]{:S(2)}) %collective-permute-start) | collective-permute-done | bytes 196640 | tf_op jit(solution)/shard_map/ppermute | solution.py:30
  224.2 3.8 multiply_convert_fusion.7
  230.8 4.2 multiply_convert_fusion.6
  338.2 3.7 fusion.7
  414.9 4.3 convolution_convert_fusion.1
  432.4 14.6 %collective-permute-done.78 = bf16[2,2,16,4736]{3,2,1,0:T(8,128)(2,1)S(1)} collective-permute-done((bf16[2,2,16,4736]{3,2,1,0:T(8,128)(2,1)S(1)}, bf16[2,2,16,4736]{3,2,1,0:T(8,128)(2,1)S(1)}, u32[]{:S(2)}, u32[]{:S(2)}) %collective-permute-start.78) | collective-permute-done | bytes 606240 | tf_op jit(solution)/shard_map/ppermute | solution.py:24
  449.7 13.7 %collective-permute-done.52 = bf16[2,2,16,4736]{3,2,1,0:T(8,128)(2,1)S(1)} collective-permute-done((bf16[2,2,16,4736]{3,2,1,0:T(8,128)(2,1)S(1)}, bf16[2,2,16,4736]{3,2,1,0:T(8,128)(2,1)S(1)}, u32[]{:S(2)}, u32[]{:S(2)}) %collective-permute-start.52) | collective-permute-done | bytes 606240 | tf_op jit(solution)/shard_map/ppermute | solution.py:24
  471.1 4.6 collective-permute-start.53
  475.6 8.3 %collective-permute-done.79 = bf16[2,2,16,4736]{3,2,1,0:T(8,128)(2,1)S(1)} collective-permute-done((bf16[2,2,16,4736]{3,2,1,0:T(8,128)(2,1)S(1)}, bf16[2,2,16,4736]{3,2,1,0:T(8,128)(2,1)S(1)}, u32[]{:S(2)}, u32[]{:S(2)}) %collective-permute-start.79) | collective-permute-done | bytes 606240 | tf_op jit(solution)/shard_map/ppermute | solution.py:24
  486.7 6.2 %collective-permute-done.86 = bf16[4,2,16,4736]{3,2,1,0:T(8,128)(2,1)S(1)} collective-permute-done((bf16[4,2,16,4736]{3,2,1,0:T(8,128)(2,1)S(1)}, bf16[4,2,16,4736]{3,2,1,0:T(8,128)(2,1)S(1)}, u32[]{:S(2)}, u32[]{:S(2)}) %collective-permute-start.86) | collective-permute-done | bytes 1212448 | tf_op jit(solution)/shard_map/ppermute | solution.py:20
  494.7 8.3 %collective-permute-done.62 = bf16[4,16,4736]{2,1,0:T(8,128)(2,1)S(1)} collective-permute-done((bf16[4,16,4736]{2,1,0:T(8,128)(2,1)S(1)}, bf16[4,16,4736]{2,1,0:T(8,128)(2,1)S(1)}, u32[]{:S(2)}, u32[]{:S(2)}) %collective-permute-start.62) | collective-permute-done | bytes 606240 | tf_op jit(solution)/shard_map/ppermute | solution.py:20
  511.1 7.6 %collective-permute-done.89 = bf16[4,16,4736]{2,1,0:T(8,128)(2,1)S(1)} collective-permute-done((bf16[4,16,4736]{2,1,0:T(8,128)(2,1)S(1)}, bf16[4,16,4736]{2,1,0:T(8,128)(2,1)S(1)}, u32[]{:S(2)}, u32[]{:S(2)}) %collective-permute-start.89) | collective-permute-done | bytes 606240 | tf_op jit(solution)/shard_map/ppermute | solution.py:20
  521.0 6.7 %collective-permute-done.63 = bf16[32,4736]{1,0:T(8,128)(2,1)S(1)} collective-permute-done((bf16[32,4736]{1,0:T(8,128)(2,1)S(1)}, bf16[32,4736]{1,0:T(8,128)(2,1)S(1)}, u32[]{:S(2)}, u32[]{:S(2)}) %collective-permute-start.63) | collective-permute-done | bytes 303136 | tf_op jit(solution)/shard_map/ppermute | solution.py:24
  529.9 8.0 %collective-permute-done.90 = bf16[32,4736]{1,0:T(8,128)(2,1)S(1)} collective-permute-done((bf16[32,4736]{1,0:T(8,128)(2,1)S(1)}, bf16[32,4736]{1,0:T(8,128)(2,1)S(1)}, u32[]{:S(2)}, u32[]{:S(2)}) %collective-permute-start.90) | collective-permute-done | bytes 303136 | tf_op jit(solution)/shard_map/ppermute | solution.py:24
  541.3 7.9 %collective-permute-done.64 = bf16[32,4736]{1,0:T(8,128)(2,1)S(1)} collective-permute-done((bf16[32,4736]{1,0:T(8,128)(2,1)S(1)}, bf16[32,4736]{1,0:T(8,128)(2,1)S(1)}, u32[]{:S(2)}, u32[]{:S(2)}) %collective-permute-start.64) | collective-permute-done | bytes 303136 | tf_op jit(solution)/shard_map/ppermute | solution.py:24
  552.6 6.8 %collective-permute-done.91 = bf16[32,4736]{1,0:T(8,128)(2,1)S(1)} collective-permute-done((bf16[32,4736]{1,0:T(8,128)(2,1)S(1)}, bf16[32,4736]{1,0:T(8,128)(2,1)S(1)}, u32[]{:S(2)}, u32[]{:S(2)}) %collective-permute-start.91) | collective-permute-done | bytes 303136 | tf_op jit(solution)/shard_map/ppermute | solution.py:24
  (848 shorter events, 375.5 us)
Async XLA Ops:
  38.6 31.8 %collective-permute-start.3 = (bf16[2,2,16,4736]{3,2,1,0:T(8,128)(2,1)S(1)}, bf16[2,2,16,4736]{3,2,1,0:T(8,128)(2,1)S(1)}, u32[]{:S(2)}, u32[]{:S(2)}) collective-permute-start(bf16[2,2,16,4736]{3,2,1,0:T(8,128)(2,1)S(1)} %pad_maximum_fusion.8), channel_id=1, source_target_pairs={{0,8},{2,10},{4,12},{6,14},{8,16},{10,18},{12,20},{14,22},{16,24},... | collective-permute-start | bytes 1818632 | tf_op jit(solution)/shard_map/ppermute | solution.py:24
  45.3 38.7 %collective-permute-start.6 = (bf16[2,2,16,4736]{3,2,1,0:T(8,128)(2,1)S(1)}, bf16[2,2,16,4736]{3,2,1,0:T(8,128)(2,1)S(1)}, u32[]{:S(2)}, u32[]{:S(2)}) collective-permute-start(bf16[2,2,16,4736]{3,2,1,0:T(8,128)(2,1)S(1)} %pad_maximum_fusion.8), channel_id=1, source_target_pairs={{24,16},{26,18},{28,20},{30,22},{16,8},{18,10},{20,12},{22,14},{8,... | collective-permute-start | bytes 1818632 | tf_op jit(solution)/shard_map/ppermute | solution.py:24
  47.3 51.9 %collective-permute-start.22 = (bf16[2,2,16,4736]{3,2,1,0:T(8,128)(2,1)S(1)}, bf16[2,2,16,4736]{3,2,1,0:T(8,128)(2,1)S(1)}, u32[]{:S(2)}, u32[]{:S(2)}) collective-permute-start(bf16[2,2,16,4736]{3,2,1,0:T(8,128)(2,1)S(1)} %pad_maximum_fusion.9), channel_id=1, source_target_pairs={{0,8},{2,10},{4,12},{6,14},{8,16},{10,18},{12,20},{14,22},{16,24},... | collective-permute-start | bytes 1818632 | tf_op jit(solution)/shard_map/ppermute | solution.py:24
  70.4 30.7 %collective-permute-start.25 = (bf16[2,2,16,4736]{3,2,1,0:T(8,128)(2,1)S(1)}, bf16[2,2,16,4736]{3,2,1,0:T(8,128)(2,1)S(1)}, u32[]{:S(2)}, u32[]{:S(2)}) collective-permute-start(bf16[2,2,16,4736]{3,2,1,0:T(8,128)(2,1)S(1)} %pad_maximum_fusion.9), channel_id=1, source_target_pairs={{24,16},{26,18},{28,20},{30,22},{16,8},{18,10},{20,12},{22,14},{8,... | collective-permute-start | bytes 1818632 | tf_op jit(solution)/shard_map/ppermute | solution.py:24
  74.8 30.3 %collective-permute-start.34 = (bf16[4,16,4736]{2,1,0:T(8,128)(2,1)S(1)}, bf16[4,16,4736]{2,1,0:T(8,128)(2,1)S(1)}, u32[]{:S(2)}, u32[]{:S(2)}) collective-permute-start(bf16[4,16,4736]{2,1,0:T(8,128)(2,1)S(1)} %get-tuple-element.196), channel_id=1, source_target_pairs={{0,2},{2,0},{4,6},{6,4},{8,10},{10,8},{12,14},{14,12},{16,18},{18,... | collective-permute-start | bytes 1818632 | tf_op jit(solution)/shard_map/ppermute | solution.py:20
  83.1 23.9 %collective-permute-start.36 = (bf16[4,16,4736]{2,1,0:T(8,128)(2,1)S(1)}, bf16[4,16,4736]{2,1,0:T(8,128)(2,1)S(1)}, u32[]{:S(2)}, u32[]{:S(2)}) collective-permute-start(bf16[4,16,4736]{2,1,0:T(8,128)(2,1)S(1)} %get-tuple-element.197), channel_id=1, source_target_pairs={{0,4},{2,6},{4,0},{6,2},{8,12},{10,14},{12,8},{14,10},{16,20},{18,... | collective-permute-start | bytes 1818632 | tf_op jit(solution)/shard_map/ppermute | solution.py:20
  84.0 29.1 %collective-permute-start.4 = (bf16[2,2,16,4736]{3,2,1,0:T(8,128)(2,1)S(1)}, bf16[2,2,16,4736]{3,2,1,0:T(8,128)(2,1)S(1)}, u32[]{:S(2)}, u32[]{:S(2)}) collective-permute-start(bf16[2,2,16,4736]{3,2,1,0:T(8,128)(2,1)S(1)} %collective-permute-done.3), channel_id=1, source_target_pairs={{8,16},{10,18},{12,20},{14,22},{16,24},{18,26},{20,28},{22,30},{9,... | collective-permute-start | bytes 1818632 | tf_op jit(solution)/shard_map/ppermute | solution.py:24
  105.1 23.0 %collective-permute-start.26 = (bf16[2,2,16,4736]{3,2,1,0:T(8,128)(2,1)S(1)}, bf16[2,2,16,4736]{3,2,1,0:T(8,128)(2,1)S(1)}, u32[]{:S(2)}, u32[]{:S(2)}) collective-permute-start(bf16[2,2,16,4736]{3,2,1,0:T(8,128)(2,1)S(1)} %collective-permute-done.25), channel_id=1, source_target_pairs={{16,8},{18,10},{20,12},{22,14},{8,0},{10,2},{12,4},{14,6},{17,9},{... | collective-permute-start | bytes 1818632 | tf_op jit(solution)/shard_map/ppermute | solution.py:24
  107.0 42.1 %collective-permute-start.16 = (bf16[2,4,16,4736]{3,2,1,0:T(8,128)(2,1)S(1)}, bf16[2,4,16,4736]{3,2,1,0:T(8,128)(2,1)S(1)}, u32[]{:S(2)}, u32[]{:S(2)}) collective-permute-start(bf16[2,4,16,4736]{3,2,1,0:T(8,128)(2,1)S(1)} %pad_maximum_fusion.3), channel_id=1, source_target_pairs={{0,4},{2,6},{4,0},{6,2},{8,12},{10,14},{12,8},{14,10},{16,20},{18,... | collective-permute-start | bytes 3637256 | tf_op jit(solution)/shard_map/ppermute | solution.py:20
  119.8 29.6 %collective-permute-start.18 = (bf16[2,4,16,4736]{3,2,0,1:T(8,128)(2,1)S(1)}, bf16[2,4,16,4736]{3,2,0,1:T(8,128)(2,1)S(1)}, u32[]{:S(2)}, u32[]{:S(2)}) collective-permute-start(bf16[2,4,16,4736]{3,2,0,1:T(8,128)(2,1)S(1)} %pad_maximum_fusion.4), channel_id=1, source_target_pairs={{0,2},{2,0},{4,6},{6,4},{8,10},{10,8},{12,14},{14,12},{16,18},{18,... | collective-permute-start | bytes 3637256 | tf_op jit(solution)/shard_map/ppermute | solution.py:20
  128.1 27.3 %collective-permute-start.35 = (bf16[2,4,16,4736]{3,2,1,0:T(8,128)(2,1)S(1)}, bf16[2,4,16,4736]{3,2,1,0:T(8,128)(2,1)S(1)}, u32[]{:S(2)}, u32[]{:S(2)}) collective-permute-start(bf16[2,4,16,4736]{3,2,1,0:T(8,128)(2,1)S(1)} %pad_maximum_fusion.6), channel_id=1, source_target_pairs={{0,4},{2,6},{4,0},{6,2},{8,12},{10,14},{12,8},{14,10},{16,20},{18,... | collective-permute-start | bytes 3637256 | tf_op jit(solution)/shard_map/ppermute | solution.py:20
  142.0 26.0 %collective-permute-start.37 = (bf16[2,4,16,4736]{3,2,1,0:T(8,128)(2,1)S(1)}, bf16[2,4,16,4736]{3,2,1,0:T(8,128)(2,1)S(1)}, u32[]{:S(2)}, u32[]{:S(2)}) collective-permute-start(bf16[2,4,16,4736]{3,2,1,0:T(8,128)(2,1)S(1)} %pad_maximum_fusion.7), channel_id=1, source_target_pairs={{0,2},{2,0},{4,6},{6,4},{8,10},{10,8},{12,14},{14,12},{16,18},{18,... | collective-permute-start | bytes 3637256 | tf_op jit(solution)/shard_map/ppermute | solution.py:20
  153.3 42.4 %collective-permute-start.19 = (bf16[768,4736]{1,0:T(8,128)(2,1)}, bf16[768,4736]{1,0:T(8,128)(2,1)}, u32[]{:S(2)}, u32[]{:S(2)}) collective-permute-start(bf16[768,4736]{1,0:T(8,128)(2,1)} %bitcast.45), channel_id=1, source_target_pairs={{0,1},{1,0},{2,3},{3,2},{4,5},{5,4},{6,7},{7,6},{8,9},{9,8},{10,11... | collective-permute-start | bytes 21823496 | tf_op jit(solution)/shard_map/ppermute | solution.py:30
  173.0 25.0 %collective-permute-start.38 = (bf16[768,4736]{1,0:T(8,128)(2,1)}, bf16[768,4736]{1,0:T(8,128)(2,1)}, u32[]{:S(2)}, u32[]{:S(2)}) collective-permute-start(bf16[768,4736]{1,0:T(8,128)(2,1)} %bitcast.656), channel_id=1, source_target_pairs={{0,1},{1,0},{2,3},{3,2},{4,5},{5,4},{6,7},{7,6},{8,9},{9,8},{10,11... | collective-permute-start | bytes 21823496 | tf_op jit(solution)/shard_map/ppermute | solution.py:30
  174.3 113.7 %collective-permute-start.40 = (bf16[128,768]{1,0:T(8,128)(2,1)}, bf16[128,768]{1,0:T(8,128)(2,1)}, u32[]{:S(2)}, u32[]{:S(2)}) collective-permute-start(bf16[128,768]{1,0:T(8,128)(2,1)} %get-tuple-element.236), channel_id=1, source_target_pairs={{0,1},{1,0},{2,3},{3,2},{4,5},{5,4},{6,7},{7,6},{8,9},{9,8},{10,11... | collective-permute-start | bytes 589832 | tf_op jit(solution)/shard_map/ppermute | solution.py:30
  377.7 24.6 %collective-permute-start.48 = (bf16[256,768]{1,0:T(8,128)(2,1)}, bf16[256,768]{1,0:T(8,128)(2,1)}, u32[]{:S(2)}, u32[]{:S(2)}) collective-permute-start(bf16[256,768]{1,0:T(8,128)(2,1)} %convert_element_type.673), channel_id=1, source_target_pairs={{0,1},{1,0},{2,3},{3,2},{4,5},{5,4},{6,7},{7,6},{8,9},{9,8},{10,11... | collective-permute-start | bytes 1179656 | tf_op jit(solution)/shard_map/ppermute | solution.py:30
  382.0 20.6 %collective-permute-start.49 = (bf16[256,1536]{1,0:T(8,128)(2,1)}, bf16[256,1536]{1,0:T(8,128)(2,1)}, u32[]{:S(2)}, u32[]{:S(2)}) collective-permute-start(bf16[256,1536]{1,0:T(8,128)(2,1)} %get-tuple-element.275), channel_id=1, source_target_pairs={{0,1},{1,0},{2,3},{3,2},{4,5},{5,4},{6,7},{7,6},{8,9},{9,8},{10,11... | collective-permute-start | bytes 2359304 | tf_op jit(solution)/shard_map/ppermute | solution.py:30
  388.5 23.0 %collective-permute-start.74 = (bf16[256,1536]{1,0:T(8,128)(2,1)}, bf16[256,1536]{1,0:T(8,128)(2,1)S(1)}, u32[]{:S(2)}, u32[]{:S(2)}) collective-permute-start(bf16[256,1536]{1,0:T(8,128)(2,1)} %fusion.5), channel_id=1, source_target_pairs={{0,1},{1,0},{2,3},{3,2},{4,5},{5,4},{6,7},{7,6},{8,9},{9,8},{10,11... | collective-permute-start | bytes 2359304 | tf_op jit(solution)/shard_map/ppermute | solution.py:30
  395.0 27.9 %collective-permute-start.75 = (bf16[256,768]{1,0:T(8,128)(2,1)}, bf16[256,768]{1,0:T(8,128)(2,1)}, u32[]{:S(2)}, u32[]{:S(2)}) collective-permute-start(bf16[256,768]{1,0:T(8,128)(2,1)} %convert_element_type.651), channel_id=1, source_target_pairs={{0,1},{1,0},{2,3},{3,2},{4,5},{5,4},{6,7},{7,6},{8,9},{9,8},{10,11... | collective-permute-start | bytes 1179656 | tf_op jit(solution)/shard_map/ppermute | solution.py:30
  396.8 27.8 %collective-permute-start.76 = (bf16[256,1536]{1,0:T(8,128)(2,1)}, bf16[256,1536]{1,0:T(8,128)(2,1)}, u32[]{:S(2)}, u32[]{:S(2)}) collective-permute-start(bf16[256,1536]{1,0:T(8,128)(2,1)} %get-tuple-element.287), channel_id=1, source_target_pairs={{0,1},{1,0},{2,3},{3,2},{4,5},{5,4},{6,7},{7,6},{8,9},{9,8},{10,11... | collective-permute-start | bytes 2359304 | tf_op jit(solution)/shard_map/ppermute | solution.py:30
  408.0 22.5 %collective-permute-start.51 = (bf16[2,2,16,4736]{3,2,1,0:T(8,128)(2,1)}, bf16[2,2,16,4736]{3,2,1,0:T(8,128)(2,1)}, u32[]{:S(2)}, u32[]{:S(2)}) collective-permute-start(bf16[2,2,16,4736]{3,2,1,0:T(8,128)(2,1)} %get-tuple-element.150), channel_id=1, source_target_pairs={{0,8},{2,10},{4,12},{6,14},{1,9},{3,11},{5,13},{7,15}} | collective-permute-start | bytes 1818632 | tf_op jit(solution)/shard_map/ppermute | solution.py:24
  411.5 37.6 %collective-permute-start.54 = (bf16[2,2,16,4736]{3,2,1,0:T(8,128)(2,1)}, bf16[2,2,16,4736]{3,2,1,0:T(8,128)(2,1)}, u32[]{:S(2)}, u32[]{:S(2)}) collective-permute-start(bf16[2,2,16,4736]{3,2,1,0:T(8,128)(2,1)} %get-tuple-element.151), channel_id=1, source_target_pairs={{24,16},{26,18},{28,20},{30,22},{25,17},{27,19},{29,21},{31,23}} | collective-permute-start | bytes 1818632 | tf_op jit(solution)/shard_map/ppermute | solution.py:24
  413.4 52.0 %collective-permute-start.61 = (bf16[4,2,16,4736]{3,2,1,0:T(8,128)(2,1)}, bf16[4,2,16,4736]{3,2,1,0:T(8,128)(2,1)}, u32[]{:S(2)}, u32[]{:S(2)}) collective-permute-start(bf16[4,2,16,4736]{3,2,1,0:T(8,128)(2,1)} %dynamic-slice_bitcast_fusion.2), channel_id=1, source_target_pairs={{0,2},{2,0},{4,6},{6,4},{8,10},{10,8},{12,14},{14,12},{16,18},{18,... | collective-permute-start | bytes 3637256 | tf_op jit(solution)/shard_map/ppermute | solution.py:20
  423.0 46.3 %collective-permute-start.59 = (bf16[4,2,16,4736]{3,2,1,0:T(8,128)(2,1)S(1)}, bf16[4,2,16,4736]{3,2,1,0:T(8,128)(2,1)S(1)}, u32[]{:S(2)}, u32[]{:S(2)}) collective-permute-start(bf16[4,2,16,4736]{3,2,1,0:T(8,128)(2,1)S(1)} %copy-done.37), channel_id=1, source_target_pairs={{0,4},{2,6},{4,0},{6,2},{8,12},{10,14},{12,8},{14,10},{16,20},{18,... | collective-permute-start | bytes 3637256 | tf_op jit(solution)/shard_map/ppermute | solution.py:20
  430.4 40.6 %collective-permute-start.81 = (bf16[2,2,16,4736]{3,2,1,0:T(8,128)(2,1)S(1)}, bf16[2,2,16,4736]{3,2,1,0:T(8,128)(2,1)S(1)}, u32[]{:S(2)}, u32[]{:S(2)}) collective-permute-start(bf16[2,2,16,4736]{3,2,1,0:T(8,128)(2,1)S(1)} %get-tuple-element.155), channel_id=1, source_target_pairs={{24,16},{26,18},{28,20},{30,22},{25,17},{27,19},{29,21},{31,23}} | collective-permute-start | bytes 1818632 | tf_op jit(solution)/shard_map/ppermute | solution.py:24
  449.1 36.7 %collective-permute-start.88 = (bf16[4,2,16,4736]{3,2,1,0:T(8,128)(2,1)S(1)}, bf16[4,2,16,4736]{3,2,1,0:T(8,128)(2,1)S(1)}, u32[]{:S(2)}, u32[]{:S(2)}) collective-permute-start(bf16[4,2,16,4736]{3,2,1,0:T(8,128)(2,1)S(1)} %dynamic-slice_bitcast_fusion), channel_id=1, source_target_pairs={{0,2},{2,0},{4,6},{6,4},{8,10},{10,8},{12,14},{14,12},{16,18},{18,... | collective-permute-start | bytes 3637256 | tf_op jit(solution)/shard_map/ppermute | solution.py:20
  463.4 29.5 %collective-permute-start.86 = (bf16[4,2,16,4736]{3,2,1,0:T(8,128)(2,1)S(1)}, bf16[4,2,16,4736]{3,2,1,0:T(8,128)(2,1)S(1)}, u32[]{:S(2)}, u32[]{:S(2)}) collective-permute-start(bf16[4,2,16,4736]{3,2,1,0:T(8,128)(2,1)S(1)} %dynamic-slice_bitcast_fusion.1), channel_id=1, source_target_pairs={{0,4},{2,6},{4,0},{6,2},{8,12},{10,14},{12,8},{14,10},{16,20},{18,... | collective-permute-start | bytes 3637256 | tf_op jit(solution)/shard_map/ppermute | solution.py:20
  469.3 37.4 %collective-permute-start.55 = (bf16[2,2,16,4736]{3,2,1,0:T(8,128)(2,1)S(1)}, bf16[2,2,16,4736]{3,2,1,0:T(8,128)(2,1)S(1)}, u32[]{:S(2)}, u32[]{:S(2)}) collective-permute-start(bf16[2,2,16,4736]{3,2,1,0:T(8,128)(2,1)S(1)} %get-tuple-element.149), channel_id=1, source_target_pairs={{24,16},{26,18},{28,20},{30,22},{16,8},{18,10},{20,12},{22,14},{25... | collective-permute-start | bytes 1818632 | tf_op jit(solution)/shard_map/ppermute | solution.py:24
  471.1 94.4 %collective-permute-start.53 = (bf16[2,2,16,4736]{3,2,1,0:T(8,128)(2,1)S(1)}, bf16[2,2,16,4736]{3,2,1,0:T(8,128)(2,1)S(1)}, u32[]{:S(2)}, u32[]{:S(2)}) collective-permute-start(bf16[2,2,16,4736]{3,2,1,0:T(8,128)(2,1)S(1)} %get-tuple-element.148), channel_id=1, source_target_pairs={{0,8},{2,10},{4,12},{6,14},{8,16},{10,18},{12,20},{14,22},{16,24},... | collective-permute-start | bytes 1818632 | tf_op jit(solution)/shard_map/ppermute | solution.py:24
  485.9 20.0 %collective-permute-start.60 = (bf16[4,16,4736]{2,1,0:T(8,128)(2,1)S(1)}, bf16[4,16,4736]{2,1,0:T(8,128)(2,1)S(1)}, u32[]{:S(2)}, u32[]{:S(2)}) collective-permute-start(bf16[4,16,4736]{2,1,0:T(8,128)(2,1)S(1)} %fusion.204), channel_id=1, source_target_pairs={{0,2},{2,0},{4,6},{6,4},{8,10},{10,8},{12,14},{14,12},{16,18},{18,... | collective-permute-start | bytes 1818632 | tf_op jit(solution)/shard_map/ppermute | solution.py:20
  503.0 68.6 %collective-permute-start.80 = (bf16[2,2,16,4736]{3,2,1,0:T(8,128)(2,1)S(1)}, bf16[2,2,16,4736]{3,2,1,0:T(8,128)(2,1)S(1)}, u32[]{:S(2)}, u32[]{:S(2)}) collective-permute-start(bf16[2,2,16,4736]{3,2,1,0:T(8,128)(2,1)S(1)} %get-tuple-element.152), channel_id=1, source_target_pairs={{0,8},{2,10},{4,12},{6,14},{8,16},{10,18},{12,20},{14,22},{16,24},... | collective-permute-start | bytes 1818632 | tf_op jit(solution)/shard_map/ppermute | solution.py:24
  507.4 61.7 %collective-permute-start.56 = (bf16[2,2,16,4736]{3,2,1,0:T(8,128)(2,1)S(1)}, bf16[2,2,16,4736]{3,2,1,0:T(8,128)(2,1)S(1)}, u32[]{:S(2)}, u32[]{:S(2)}) collective-permute-start(bf16[2,2,16,4736]{3,2,1,0:T(8,128)(2,1)S(1)} %fusion.125), channel_id=1, source_target_pairs={{24,16},{26,18},{28,20},{30,22},{16,8},{18,10},{20,12},{22,14},{8,... | collective-permute-start | bytes 1818632 | tf_op jit(solution)/shard_map/ppermute | solution.py:24
  (212 other events, 1421.6 us)
